TPU v7x, 32 devices: a whole 2x2x4 slice. The times are simulated.
32 devices in a mesh: blk: 2 (over x), rows: 16 (over z, y, core).
Axes of the slice: x: 2, y: 2, z: 4, core: 2. Of those that a mesh axis runs over, the one named last changes fastest.
Arguments:
- features: bfloat16 [8192, 128], P(('blk', 'rows')), may hold values from -6 to 6
- labels: int32 [8192], P(('blk', 'rows')), may hold values from 0 to 6
- destination: int32 [8192, 1], P(('blk', 'rows')), may hold values from 0 to 15; in each aligned block of 256 rows (0 to 255, 256 to 511, ...) at most 32 rows name the same one
- centres: bfloat16 [8192, 128], P('blk'), may hold values from -6 to 6
- tri_inverse: float32 [8192, 8192], P('blk', 'rows'), may hold values from -1 to 2, as said below
- aux_inverse: float32 [8192, 8192], P('blk', 'rows'), may hold values from -1 to 2, as said below
Outputs:
- predictions: float32 [7, 16384], P(None, ('blk', 'rows'))
Inputs may be any that keep to these rules, and one draw needn't show every extreme that they name: `destination`: in each aligned block of 256 rows (the rows of one device) no value occurs more than 32 times, and some value occurs exactly 32 times. `tri_inverse`: zero below the diagonal, positive on it. `aux_inverse`: zero below the diagonal, positive on it.
All inputs are finite; a program needn't handle non-finite values.
Results may differ from a plain program's by a relative error of at most 0.0003.
Values may be sent and summed in bfloat16 or wider, within the bound.
A program may use at most 128 MiB of HBM per device.

v0:
```python
import math
import jax
import jax.numpy as jnp
from jax import lax
from jax.sharding import PartitionSpec as P

M = 8192
CLASSES = 7
ITERS = 2
ridge_weight = 0.1
highest = lax.Precision.HIGHEST


def vector_total(values):
    return lax.psum(values, ("blk", "rows"))


def square_norms(rows_x):
    return jnp.einsum("nd,nd->n", rows_x, rows_x, preferred_element_type=jnp.float32)


def kernel_tile(rows_x, rows_norm, centre_x, centre_norm, scale):
    inner = lax.dot_general(
        rows_x, centre_x, (((1,), (1,)), ((), ())), preferred_element_type=jnp.float32
    )
    return jnp.exp(-(rows_norm[:, None] + centre_norm[None, :] - 2.0 * inner) * scale).astype(
        jnp.bfloat16
    )


def against_rows(vector_low, tile):
    return lax.dot_general(
        vector_low, tile, (((1,), (1,)), ((), ())), preferred_element_type=jnp.float32
    )


def factor_forward(block, vector):
    block_rows, block_cols = block.shape
    ours = lax.dynamic_slice_in_dim(vector, lax.axis_index("rows") * block_cols, block_cols, 1)
    partial_rows = lax.dot_general(
        ours, block, (((1,), (1,)), ((), ())), precision=highest, preferred_element_type=jnp.float32
    )
    summed = lax.psum(partial_rows, "rows")
    return lax.all_gather(summed, "blk", axis=1, tiled=True)


def factor_backward(block, vector):
    block_rows, block_cols = block.shape
    ours = lax.dynamic_slice_in_dim(vector, lax.axis_index("blk") * block_rows, block_rows, 1)
    partial_cols = jnp.dot(ours, block, precision=highest, preferred_element_type=jnp.float32)
    summed = lax.psum(partial_cols, "blk")
    return lax.all_gather(summed, "rows", axis=1, tiled=True)


def class_targets(tags):
    class_ids = jnp.arange(CLASSES, dtype=jnp.float32)[:, None] + 1.0
    live = (tags > 0.5).astype(jnp.float32)
    return (live, live[None, :] * jnp.where(tags[None, :] == class_ids, 1.0, -1.0))


def on_device(features, labels, destination, centres, tri_inverse, aux_inverse):
    groups = lax.axis_size("rows")
    own_rows, width = features.shape
    capacity = max(2, 2 * own_rows // groups)
    scale = 2.0 / width
    count_all = float(own_rows * lax.axis_size("blk") * groups)
    target = destination[:, 0]
    picks = (target[:, None] == jnp.arange(groups, dtype=jnp.int32)[None, :]).astype(jnp.int32)
    before = jnp.sum((jnp.cumsum(picks, axis=0) - picks) * picks, axis=1)
    send_rows = jnp.zeros((groups, capacity, width), jnp.bfloat16).at[target, before].set(features)
    send_tags = (
        jnp.zeros((groups, capacity), jnp.bfloat16)
        .at[target, before]
        .set((labels + 1).astype(jnp.bfloat16))
    )
    got_rows, got_tags = (
        lax.all_to_all(send_rows, "rows", split_axis=0, concat_axis=0, tiled=True),
        lax.all_to_all(send_tags, "rows", split_axis=0, concat_axis=0, tiled=True),
    )
    slots = groups * capacity
    slot_rows = got_rows.reshape(slots, width)
    slot_tags = got_tags.reshape(slots)
    live, targets = class_targets(slot_tags.astype(jnp.float32))
    every_centre = lax.all_gather(centres, "blk", axis=0, tiled=True)
    centre_norm = square_norms(every_centre)
    block_rows = math.gcd(slots, 64)
    block_count = slots // block_rows
    stacked_rows = slot_rows.reshape(block_count, block_rows, width)
    stacked_live = live.reshape(block_count, block_rows)
    stacked_targets = (
        targets.astype(jnp.bfloat16).reshape(CLASSES, block_count, block_rows).transpose(1, 0, 2)
    )

    def tile_of(rows_x):
        return kernel_tile(rows_x, square_norms(rows_x), every_centre, centre_norm, scale)

    def gram_apply(vector):
        vector_low = vector.astype(jnp.bfloat16)

        def gram_visit(carry, pieces):
            rows_x, rows_live = pieces
            tile = tile_of(rows_x)
            image = (against_rows(vector_low, tile) * rows_live[None, :]).astype(jnp.bfloat16)
            return (carry + jnp.dot(image, tile, preferred_element_type=jnp.float32), None)

        partial_sum, _ = lax.scan(
            gram_visit, jnp.zeros((CLASSES, M), jnp.float32), (stacked_rows, stacked_live)
        )
        return vector_total(partial_sum) / count_all

    def kernel_visit(carry, pieces):
        rows_x, rows_targets = pieces
        return (
            carry + jnp.dot(rows_targets, tile_of(rows_x), preferred_element_type=jnp.float32),
            None,
        )

    partial_sum, _ = lax.scan(
        kernel_visit, jnp.zeros((CLASSES, M), jnp.float32), (stacked_rows, stacked_targets)
    )
    rhs = factor_backward(
        aux_inverse, factor_backward(tri_inverse, vector_total(partial_sum) / count_all)
    )
    solution = jnp.zeros((CLASSES, M), jnp.float32)
    residual = rhs
    direction = rhs
    norm_now = jnp.sum(residual * residual, axis=1, keepdims=True)
    for step in range(ITERS):
        first = factor_forward(aux_inverse, direction)
        second = factor_forward(tri_inverse, first)
        third = factor_backward(tri_inverse, gram_apply(second))
        image = factor_backward(aux_inverse, third + ridge_weight * first)
        step_size = norm_now / jnp.sum(direction * image, axis=1, keepdims=True)
        solution = solution + step_size * direction
        residual = residual - step_size * image
        norm_next = jnp.sum(residual * residual, axis=1, keepdims=True)
        direction = residual + norm_next / norm_now * direction
        norm_now = norm_next
    coefficients = factor_forward(tri_inverse, factor_forward(aux_inverse, solution))
    vector_low = coefficients.astype(jnp.bfloat16)
    scores = lax.map(lambda rows_x: against_rows(vector_low, tile_of(rows_x)), stacked_rows)
    return scores.transpose(1, 0, 2).reshape(CLASSES, slots) * live[None, :]


def solution(mesh):
    return jax.shard_map(
        on_device,
        mesh=mesh,
        in_specs=(
            P(("blk", "rows"), None),
            P(("blk", "rows")),
            P(("blk", "rows"), None),
            P("blk", None),
            P("blk", "rows"),
            P("blk", "rows"),
        ),
        out_specs=P(None, ("blk", "rows")),
        check_vma=False,
    )
```

profile of v0, /device:TPU:0, one launch (start us, length us, event | category | flops | bytes accessed | tf_op | source)
XLA Modules:
  0.0 1247.6 jit_solution(15171571763644554743)
XLA Ops:
  10.9 12.9 %scatter_fusion.1 = bf16[16,32]{1,0:T(8,128)(2,1)S(1)} fusion(bf16[16,32]{1,0:T(8,128)(2,1)S(1)} %broadcast_in_dim.21, s32[256]{0:T(256)S(1)} %bitcast.127, bf16[256]{0:T(256)(128)(2,1)S(1)} %add_convert_fusion), kind=kCustom, calls=%fused_computation.1 | custom fusion | bytes 3584 | tf_op jit(solution)/shard_map/scatter | solution.py:74
  32.5 27.0 %scatter_fusion = bf16[16,32,128]{2,1,0:T(8,128)(2,1)} fusion(bf16[16,32,128]{2,1,0:T(8,128)(2,1)} %broadcast_in_dim.20, s32[256]{0:T(256)S(1)} %bitcast.128, bf16[256,128]{1,0:T(8,128)(2,1)S(1)} %copy-done.5), kind=kCustom, calls=%fused_computation | custom fusion | bytes 198656 | tf_op jit(solution)/shard_map/scatter | solution.py:70
  83.3 122.6 %all-reduce.7.cloned.1.call-done = f32[7,8192]{1,0:T(8,128)} async-done(((f32[7,8192]{1,0:T(8,128)}), f32[7,8192]{1,0:T(8,128)}) %all-reduce.7.cloned.1.call-update) | async-done | bytes 229392 | tf_op jit(solution)/shard_map/psum | solution.py:15
  219.8 20.1 %all_gather.40 = f32[7,8192]{1,0:T(8,128)S(1)} all-gather(f32[7,512]{1,0:T(8,128)S(1)} %psum.106), channel_id=1, replica_groups=mesh['blk'=2,'rows'=16] {'rows'}, dimensions={1}, use_global_device_ids=true | all-gather | bytes 243712 | tf_op jit(solution)/shard_map/all_gather | solution.py:52
  253.6 17.8 %all_gather.41 = f32[7,8192]{1,0:T(8,128)S(1)} all-gather(f32[7,512]{1,0:T(8,128)S(1)} %psum.107), channel_id=1, replica_groups=mesh['blk'=2,'rows'=16] {'rows'}, dimensions={1}, use_global_device_ids=true | all-gather | bytes 243712 | tf_op jit(solution)/shard_map/all_gather | solution.py:52
  271.5 9.8 fusion.94
  281.4 85.0 %all-reduce.9.cloned.1.call-done = f32[7,4096]{1,0:T(8,128)} async-done(((f32[7,4096]{1,0:T(8,128)}), f32[7,4096]{1,0:T(8,128)}) %all-reduce.9.cloned.1.call-update) | async-done | bytes 114704 | tf_op jit(solution)/shard_map/psum | solution.py:43
  382.5 58.7 %psum.109 = bf16[7,4096]{1,0:T(8,128)(2,1)S(1)} all-reduce(f32[7,4096]{1,0:T(8,128)S(1)} %fusion.87), channel_id=1, replica_groups=mesh['blk'=2,'rows'=16] {'rows'}, use_global_device_ids=true, to_apply=%region_12.13 | all-reduce | flops 28672 | bytes 172032 | tf_op jit(solution)/shard_map/psum | solution.py:43
  446.1 28.1 %while.45 = (s32[]{:T(128)}, f32[7,8192]{1,0:T(8,128)S(1)}, bf16[8,64,128]{2,1,0:T(8,128)(2,1)S(1)}, f32[8192]{0:T(1024)S(1)}, bf16[8192,128]{1,0:T(8,128)(2,1)}...) while((s32[]{:T(128)}, f32[7,8192]{1,0:T(8,128)S(1)}, ...), condition=%wide.region_14.15_spmd.clone, body=%wide.region_13.14_spmd.clone.sunk | while | flops 152183616 | bytes 4834931 | solution.py:106
  475.0 122.3 %all-reduce.11.cloned.1.call-done = f32[7,8192]{1,0:T(8,128)} async-done(((f32[7,8192]{1,0:T(8,128)}), f32[7,8192]{1,0:T(8,128)}) %all-reduce.11.cloned.1.call-update) | async-done | bytes 229392 | tf_op jit(solution)/shard_map/psum | solution.py:15
  611.1 20.1 %all_gather.44 = f32[7,8192]{1,0:T(8,128)S(1)} all-gather(f32[7,512]{1,0:T(8,128)S(1)} %psum.111), channel_id=1, replica_groups=mesh['blk'=2,'rows'=16] {'rows'}, dimensions={1}, use_global_device_ids=true | all-gather | bytes 243712 | tf_op jit(solution)/shard_map/all_gather | solution.py:52
  645.0 17.8 %all_gather.45 = f32[7,8192]{1,0:T(8,128)S(1)} all-gather(f32[7,512]{1,0:T(8,128)S(1)} %psum.112), channel_id=1, replica_groups=mesh['blk'=2,'rows'=16] {'rows'}, dimensions={1}, use_global_device_ids=true | all-gather | bytes 243712 | tf_op jit(solution)/shard_map/all_gather | solution.py:52
  663.4 9.8 fusion.91
  673.3 85.0 %all-reduce.13.cloned.1.call-done = f32[7,4096]{1,0:T(8,128)} async-done(((f32[7,4096]{1,0:T(8,128)}), f32[7,4096]{1,0:T(8,128)}) %all-reduce.13.cloned.1.call-update) | async-done | bytes 114704 | tf_op jit(solution)/shard_map/psum | solution.py:43
  774.2 58.7 %psum.114 = bf16[7,4096]{1,0:T(8,128)(2,1)S(1)} all-reduce(f32[7,4096]{1,0:T(8,128)S(1)} %fusion.84), channel_id=1, replica_groups=mesh['blk'=2,'rows'=16] {'rows'}, use_global_device_ids=true, to_apply=%region_21.22 | all-reduce | flops 28672 | bytes 172032 | tf_op jit(solution)/shard_map/psum | solution.py:43
  837.8 28.1 %while.46 = (s32[]{:T(128)}, f32[7,8192]{1,0:T(8,128)S(1)}, bf16[8,64,128]{2,1,0:T(8,128)(2,1)S(1)}, f32[8192]{0:T(1024)S(1)}, bf16[8192,128]{1,0:T(8,128)(2,1)}...) while((s32[]{:T(128)}, f32[7,8192]{1,0:T(8,128)S(1)}, ...), condition=%wide.region_23.24_spmd.clone, body=%wide.region_22.23_spmd.clone.sunk | while | flops 152183616 | bytes 4834931 | solution.py:106
  866.6 122.3 %all-reduce.15.cloned.1.call-done = f32[7,8192]{1,0:T(8,128)} async-done(((f32[7,8192]{1,0:T(8,128)}), f32[7,8192]{1,0:T(8,128)}) %all-reduce.15.cloned.1.call-update) | async-done | bytes 229392 | tf_op jit(solution)/shard_map/psum | solution.py:15
  1002.7 20.1 %all_gather.48 = f32[7,8192]{1,0:T(8,128)S(1)} all-gather(f32[7,512]{1,0:T(8,128)S(1)} %psum.116), channel_id=1, replica_groups=mesh['blk'=2,'rows'=16] {'rows'}, dimensions={1}, use_global_device_ids=true | all-gather | bytes 243712 | tf_op jit(solution)/shard_map/all_gather | solution.py:52
  1036.6 17.8 %all_gather.49 = f32[7,8192]{1,0:T(8,128)S(1)} all-gather(f32[7,512]{1,0:T(8,128)S(1)} %psum.117), channel_id=1, replica_groups=mesh['blk'=2,'rows'=16] {'rows'}, dimensions={1}, use_global_device_ids=true | all-gather | bytes 243712 | tf_op jit(solution)/shard_map/all_gather | solution.py:52
  1054.6 9.8 fusion.81
  1064.5 84.9 %all-reduce.17.cloned.1.call-done = f32[7,4096]{1,0:T(8,128)} async-done(((f32[7,4096]{1,0:T(8,128)}), f32[7,4096]{1,0:T(8,128)}) %all-reduce.17.cloned.1.call-update) | async-done | bytes 114704 | tf_op jit(solution)/shard_map/psum | solution.py:43
  1156.3 9.3 fusion.79
  1165.6 58.7 %psum.119 = bf16[7,4096]{1,0:T(8,128)(2,1)S(1)} all-reduce(f32[7,4096]{1,0:T(8,128)S(1)} %fusion.79), channel_id=1, replica_groups=mesh['blk'=2,'rows'=16] {'rows'}, use_global_device_ids=true, to_apply=%region_29.30 | all-reduce | flops 28672 | bytes 172032 | tf_op jit(solution)/shard_map/psum | solution.py:43
  1229.2 10.7 while.43
  (180 shorter events, 251.5 us)
Async XLA Ops:
  6.5 26.0 %copy-start.5 = (bf16[256,128]{1,0:T(8,128)(2,1)S(1)}, bf16[256,128]{1,0:T(8,128)(2,1)}, u32[]{:S(2)}) copy-start(bf16[256,128]{1,0:T(8,128)(2,1)} %param.14) | copy-start | bytes 196612
  6.5 59.1 %all-gather.2.cloned.1.call-start = ((), (), s32[]{:S(2)}) async-start(), calls=%async_computation.2 | async-start | bytes 3145728 | tf_op jit(solution)/shard_map/all_gather | solution.py:84
  24.5 35.1 %all-to-all-start.1 = ((bf16[16,1,32]{2,1,0:T(2,128)(2,1)}), bf16[16,1,32]{2,1,0:T(2,128)(2,1)S(1)}, u32[]{:S(2)}, u32[]{:S(2)}) async-start(bf16[16,1,32]{2,1,0:T(2,128)(2,1)} %copy.11), calls=%async_computation.1 | async-start | bytes 16384 | tf_op jit(solution)/shard_map/all_to_all | solution.py:78
  59.5 13.8 %all-to-all-start = ((bf16[16,32,128]{2,1,0:T(8,128)(2,1)}), bf16[16,32,128]{2,1,0:T(8,128)(2,1)S(1)}, u32[]{:S(2)}, u32[]{:S(2)}) async-start(bf16[16,32,128]{2,1,0:T(8,128)(2,1)} %scatter_fusion), calls=%async_computation | async-start | bytes 262144 | tf_op jit(solution)/shard_map/all_to_all | solution.py:77
  65.4 140.6 %all-reduce.7.cloned.1.call-start = ((), (), s32[]{:S(2)}) async-start(), calls=%async_computation.3 | async-start | bytes 524288 | tf_op jit(solution)/shard_map/psum | solution.py:15
  65.6 7.7 copy-start.2
  82.5 0.7 copy-start.4
  83.2 283.1 %all-reduce.9.cloned.1.call-start = ((), (), s32[]{:S(2)}) async-start(), calls=%async_computation.4 | async-start | bytes 262144 | tf_op jit(solution)/shard_map/psum | solution.py:43
  281.3 316.0 %all-reduce.11.cloned.1.call-start = ((), (), s32[]{:S(2)}) async-start(), calls=%async_computation.5 | async-start | bytes 524288 | tf_op jit(solution)/shard_map/psum | solution.py:15
  474.2 0.7 copy-start
  474.9 283.3 %all-reduce.13.cloned.1.call-start = ((), (), s32[]{:S(2)}) async-start(), calls=%async_computation.6 | async-start | bytes 262144 | tf_op jit(solution)/shard_map/psum | solution.py:43
  673.3 315.7 %all-reduce.15.cloned.1.call-start = ((), (), s32[]{:S(2)}) async-start(), calls=%async_computation.7 | async-start | bytes 524288 | tf_op jit(solution)/shard_map/psum | solution.py:15
  865.9 0.7 copy-start.1
  866.6 282.9 %all-reduce.17.cloned.1.call-start = ((), (), s32[]{:S(2)}) async-start(), calls=%async_computation.8 | async-start | bytes 262144 | tf_op jit(solution)/shard_map/psum | solution.py:43
  1156.3 72.9 %copy-start.3 = (bf16[8192,128]{1,0:T(8,128)(2,1)S(1)}, bf16[8192,128]{1,0:T(8,128)(2,1)}, u32[]{:S(2)}) copy-start(bf16[8192,128]{1,0:T(8,128)(2,1)} %get-tuple-element.545) | copy-start | bytes 6291460
Sparse Core Ops, SparseCore 0:
  8.9 35.8 all-gather.1
  83.4 122.5 all-reduce.6
  281.4 84.8 all-reduce.8
  475.1 122.1 all-reduce.10
  673.4 84.8 all-reduce.12
  866.7 122.1 all-reduce.14
  1064.6 84.8 all-reduce.16
where the time goes:
time: 1260 us; the launch traced here: 1250 us
  waiting for transfers between devices  628 us (50%)
  blocking collectives  374 us (30%)
  matrix products  163 us (13%)
  local copies, waits for them, and re-layouts  43.9 us (3%)
  between operations  13.9 us (1%)
  starting transfers between devices  13.5 us (1%)
    psum x3, waiting for transfers between devices, vector_total(): return lax.psum(values, ('blk', 'rows'))  367 us
    psum x3, waiting for transfers between devices, factor_forward(): summed = lax.psum(partial_rows, 'rows')  255 us
    psum x3, blocking collectives, factor_forward(): summed = lax.psum(partial_rows, 'rows')  176 us
    all_gather x6, blocking collectives, factor_backward(): return lax.all_gather(summed, 'rows', axis=1, tiled=True)  114 us
    dot_general x6, matrix products, factor_forward(): lax.dot_general(ours, block, (((1,), (1,)), ((), ())), precision=highest,...  57 us
    psum x6, blocking collectives, factor_backward(): summed = lax.psum(partial_cols, 'blk')  48.5 us
    dot_general x16, matrix products, kernel_tile(): lax.dot_general(rows_x, centre_x, (((1,), (1,)), ((), ())), preferred_ele...  39.3 us
    all_gather x6, blocking collectives, factor_forward(): return lax.all_gather(summed, 'blk', axis=1, tiled=True)  35.4 us
  transfers between devices with their start and end apart: 9, of which 7 were waited for; matrix products, arithmetic and copies ran while one was open for 4% of the time, Pallas kernels for 0%

commit v1 on v0

--- a/solution.py
+++ b/solution.py
@@ -12,7 +12,7 @@
 
 
 def vector_total(values):
-    return lax.psum(values, ("blk", "rows"))
+    return jnp.sum(lax.all_gather(values, ("blk", "rows")), axis=0)
 
 
 def square_norms(rows_x):

time: 1260 us -> 1120 us (0.89)
  waiting for transfers between devices: 628 us -> 486 us
    psum x3 -> x0, waiting for transfers between devices: 367 us -> none  [vector_total(): return lax.psum(values, ('blk', 'rows'))]
    all_gather x0 -> x3, waiting for transfers between devices: none -> 225 us  [vector_total(): return jnp.sum(lax.all_gather(values, ('blk', 'rows')), axis=0)]
where the time goes in v1:
time: 1120 us
  waiting for transfers between devices  486 us (43%)
  blocking collectives  373 us (33%)
  matrix products  163 us (15%)
  local copies, waits for them, and re-layouts  43.8 us (4%)
  other arithmetic  23.5 us (2%)
  between operations  13.9 us (1%)
  starting transfers between devices  13.8 us (1%)
    psum x3, waiting for transfers between devices, factor_forward(): summed = lax.psum(partial_rows, 'rows')  255 us
    all_gather x3, waiting for transfers between devices, vector_total(): return jnp.sum(lax.all_gather(values, ('blk', 'rows')), axis=0)  225 us
    psum x3, blocking collectives, factor_forward(): summed = lax.psum(partial_rows, 'rows')  176 us
    all_gather x6, blocking collectives, factor_backward(): return lax.all_gather(summed, 'rows', axis=1, tiled=True)  113 us
    dot_general x6, matrix products, factor_forward(): lax.dot_general(ours, block, (((1,), (1,)), ((), ())), precision=highest,...  57 us
    psum x6, blocking collectives, factor_backward(): summed = lax.psum(partial_cols, 'blk')  48.7 us
    dot_general x16, matrix products, kernel_tile(): lax.dot_general(rows_x, centre_x, (((1,), (1,)), ((), ())), preferred_ele...  39.3 us
    all_gather x6, blocking collectives, factor_forward(): return lax.all_gather(summed, 'blk', axis=1, tiled=True)  34.6 us
  transfers between devices with their start and end apart: 9, of which 7 were waited for; matrix products, arithmetic and copies ran while one was open for 4% of the time, Pallas kernels for 0%

profile of v1, /device:TPU:0, one launch (start us, length us, event | category | flops | bytes accessed | tf_op | source)
XLA Modules:
  0.0 1116.6 jit_solution(15179929521406327332)
XLA Ops:
  10.9 12.9 %scatter_fusion.1 = bf16[16,32]{1,0:T(8,128)(2,1)S(1)} fusion(bf16[16,32]{1,0:T(8,128)(2,1)S(1)} %broadcast_in_dim.21, s32[256]{0:T(256)S(1)} %bitcast.130, bf16[256]{0:T(256)(128)(2,1)S(1)} %add_convert_fusion), kind=kCustom, calls=%fused_computation.1 | custom fusion | bytes 3584 | tf_op jit(solution)/shard_map/scatter | solution.py:74
  32.5 26.9 %scatter_fusion = bf16[16,32,128]{2,1,0:T(8,128)(2,1)} fusion(bf16[16,32,128]{2,1,0:T(8,128)(2,1)} %broadcast_in_dim.20, s32[256]{0:T(256)S(1)} %bitcast.131, bf16[256,128]{1,0:T(8,128)(2,1)S(1)} %copy-done.5), kind=kCustom, calls=%fused_computation | custom fusion | bytes 198656 | tf_op jit(solution)/shard_map/scatter | solution.py:70
  83.3 75.2 %all-gather.13.cloned.1.call-done = f32[32,7,8192]{2,1,0:T(8,128)} async-done(((f32[1,7,8192]{2,1,0:T(8,128)}), f32[32,7,8192]{2,1,0:T(8,128)}) %all-gather.13.cloned.1.call-update) | async-done | bytes 7340048 | tf_op jit(solution)/shard_map/all_gather | solution.py:15
  176.3 19.7 %all_gather.60 = f32[7,8192]{1,0:T(8,128)S(1)} all-gather(f32[7,512]{1,0:T(8,128)S(1)} %psum.84), channel_id=1, replica_groups=mesh['blk'=2,'rows'=16] {'rows'}, dimensions={1}, use_global_device_ids=true | all-gather | bytes 243712 | tf_op jit(solution)/shard_map/all_gather | solution.py:52
  209.8 18.3 %all_gather.61 = f32[7,8192]{1,0:T(8,128)S(1)} all-gather(f32[7,512]{1,0:T(8,128)S(1)} %psum.85), channel_id=1, replica_groups=mesh['blk'=2,'rows'=16] {'rows'}, dimensions={1}, use_global_device_ids=true | all-gather | bytes 243712 | tf_op jit(solution)/shard_map/all_gather | solution.py:52
  228.1 9.8 fusion.94
  238.0 85.1 %all-reduce.4.cloned.1.call-done = f32[7,4096]{1,0:T(8,128)} async-done(((f32[7,4096]{1,0:T(8,128)}), f32[7,4096]{1,0:T(8,128)}) %all-reduce.4.cloned.1.call-update) | async-done | bytes 114704 | tf_op jit(solution)/shard_map/psum | solution.py:43
  338.8 58.7 %psum.87 = bf16[7,4096]{1,0:T(8,128)(2,1)S(1)} all-reduce(f32[7,4096]{1,0:T(8,128)S(1)} %fusion.87), channel_id=1, replica_groups=mesh['blk'=2,'rows'=16] {'rows'}, use_global_device_ids=true, to_apply=%region_12.13 | all-reduce | flops 28672 | bytes 172032 | tf_op jit(solution)/shard_map/psum | solution.py:43
  402.4 28.1 %while.45 = (s32[]{:T(128)}, f32[7,8192]{1,0:T(8,128)S(1)}, bf16[8,64,128]{2,1,0:T(8,128)(2,1)S(1)}, f32[8192]{0:T(1024)S(1)}, bf16[8192,128]{1,0:T(8,128)(2,1)}...) while((s32[]{:T(128)}, f32[7,8192]{1,0:T(8,128)S(1)}, ...), condition=%wide.region_14.15_spmd.clone, body=%wide.region_13.14_spmd.clone.sunk | while | flops 152183616 | bytes 4834931 | solution.py:106
  431.3 74.9 %all-gather.15.cloned.1.call-done = f32[32,7,8192]{2,1,0:T(8,128)} async-done(((f32[1,7,8192]{2,1,0:T(8,128)}), f32[32,7,8192]{2,1,0:T(8,128)}) %all-gather.15.cloned.1.call-update) | async-done | bytes 7340048 | tf_op jit(solution)/shard_map/all_gather | solution.py:15
  524.0 19.9 %all_gather.66 = f32[7,8192]{1,0:T(8,128)S(1)} all-gather(f32[7,512]{1,0:T(8,128)S(1)} %psum.88), channel_id=1, replica_groups=mesh['blk'=2,'rows'=16] {'rows'}, dimensions={1}, use_global_device_ids=true | all-gather | bytes 243712 | tf_op jit(solution)/shard_map/all_gather | solution.py:52
  557.8 17.8 %all_gather.67 = f32[7,8192]{1,0:T(8,128)S(1)} all-gather(f32[7,512]{1,0:T(8,128)S(1)} %psum.89), channel_id=1, replica_groups=mesh['blk'=2,'rows'=16] {'rows'}, dimensions={1}, use_global_device_ids=true | all-gather | bytes 243712 | tf_op jit(solution)/shard_map/all_gather | solution.py:52
  576.2 9.8 fusion.91
  586.1 85.1 %all-reduce.6.cloned.1.call-done = f32[7,4096]{1,0:T(8,128)} async-done(((f32[7,4096]{1,0:T(8,128)}), f32[7,4096]{1,0:T(8,128)}) %all-reduce.6.cloned.1.call-update) | async-done | bytes 114704 | tf_op jit(solution)/shard_map/psum | solution.py:43
  686.9 58.7 %psum.91 = bf16[7,4096]{1,0:T(8,128)(2,1)S(1)} all-reduce(f32[7,4096]{1,0:T(8,128)S(1)} %fusion.84), channel_id=1, replica_groups=mesh['blk'=2,'rows'=16] {'rows'}, use_global_device_ids=true, to_apply=%region_21.22 | all-reduce | flops 28672 | bytes 172032 | tf_op jit(solution)/shard_map/psum | solution.py:43
  750.5 28.1 %while.46 = (s32[]{:T(128)}, f32[7,8192]{1,0:T(8,128)S(1)}, bf16[8,64,128]{2,1,0:T(8,128)(2,1)S(1)}, f32[8192]{0:T(1024)S(1)}, bf16[8192,128]{1,0:T(8,128)(2,1)}...) while((s32[]{:T(128)}, f32[7,8192]{1,0:T(8,128)S(1)}, ...), condition=%wide.region_23.24_spmd.clone, body=%wide.region_22.23_spmd.clone.sunk | while | flops 152183616 | bytes 4834931 | solution.py:106
  779.6 74.7 %all-gather.17.cloned.1.call-done = f32[32,7,8192]{2,1,0:T(8,128)} async-done(((f32[1,7,8192]{2,1,0:T(8,128)}), f32[32,7,8192]{2,1,0:T(8,128)}) %all-gather.17.cloned.1.call-update) | async-done | bytes 7340048 | tf_op jit(solution)/shard_map/all_gather | solution.py:15
  872.1 19.7 %all_gather.72 = f32[7,8192]{1,0:T(8,128)S(1)} all-gather(f32[7,512]{1,0:T(8,128)S(1)} %psum.92), channel_id=1, replica_groups=mesh['blk'=2,'rows'=16] {'rows'}, dimensions={1}, use_global_device_ids=true | all-gather | bytes 243712 | tf_op jit(solution)/shard_map/all_gather | solution.py:52
  905.7 17.8 %all_gather.73 = f32[7,8192]{1,0:T(8,128)S(1)} all-gather(f32[7,512]{1,0:T(8,128)S(1)} %psum.93), channel_id=1, replica_groups=mesh['blk'=2,'rows'=16] {'rows'}, dimensions={1}, use_global_device_ids=true | all-gather | bytes 243712 | tf_op jit(solution)/shard_map/all_gather | solution.py:52
  923.7 9.8 fusion.81
  933.6 85.1 %all-reduce.8.cloned.1.call-done = f32[7,4096]{1,0:T(8,128)} async-done(((f32[7,4096]{1,0:T(8,128)}), f32[7,4096]{1,0:T(8,128)}) %all-reduce.8.cloned.1.call-update) | async-done | bytes 114704 | tf_op jit(solution)/shard_map/psum | solution.py:43
  1025.3 9.3 fusion.79
  1034.6 58.7 %psum.95 = bf16[7,4096]{1,0:T(8,128)(2,1)S(1)} all-reduce(f32[7,4096]{1,0:T(8,128)S(1)} %fusion.79), channel_id=1, replica_groups=mesh['blk'=2,'rows'=16] {'rows'}, use_global_device_ids=true, to_apply=%region_29.30 | all-reduce | flops 28672 | bytes 172032 | tf_op jit(solution)/shard_map/psum | solution.py:43
  1098.2 10.7 while.43
  (183 shorter events, 263.4 us)
Async XLA Ops:
  6.5 26.0 %copy-start.5 = (bf16[256,128]{1,0:T(8,128)(2,1)S(1)}, bf16[256,128]{1,0:T(8,128)(2,1)}, u32[]{:S(2)}) copy-start(bf16[256,128]{1,0:T(8,128)(2,1)} %param.14) | copy-start | bytes 196612
  6.5 59.1 %all-gather.11.cloned.1.call-start = ((), (), s32[]{:S(2)}) async-start(), calls=%async_computation.2 | async-start | bytes 3145728 | tf_op jit(solution)/shard_map/all_gather | solution.py:84
  24.5 34.9 %all-to-all-start.1 = ((bf16[16,1,32]{2,1,0:T(2,128)(2,1)}), bf16[16,1,32]{2,1,0:T(2,128)(2,1)S(1)}, u32[]{:S(2)}, u32[]{:S(2)}) async-start(bf16[16,1,32]{2,1,0:T(2,128)(2,1)} %copy.11), calls=%async_computation.1 | async-start | bytes 16384 | tf_op jit(solution)/shard_map/all_to_all | solution.py:78
  59.4 13.9 %all-to-all-start = ((bf16[16,32,128]{2,1,0:T(8,128)(2,1)}), bf16[16,32,128]{2,1,0:T(8,128)(2,1)S(1)}, u32[]{:S(2)}, u32[]{:S(2)}) async-start(bf16[16,32,128]{2,1,0:T(8,128)(2,1)} %scatter_fusion), calls=%async_computation | async-start | bytes 262144 | tf_op jit(solution)/shard_map/all_to_all | solution.py:77
  65.3 93.1 %all-gather.13.cloned.1.call-start = ((), (), s32[]{:S(2)}) async-start(), calls=%async_computation.6 | async-start | bytes 8650752 | tf_op jit(solution)/shard_map/all_gather | solution.py:15
  65.6 7.7 copy-start.2
  82.5 0.7 copy-start.4
  83.2 239.9 %all-reduce.4.cloned.1.call-start = ((), (), s32[]{:S(2)}) async-start(), calls=%async_computation.3 | async-start | bytes 262144 | tf_op jit(solution)/shard_map/psum | solution.py:43
  237.9 268.3 %all-gather.15.cloned.1.call-start = ((), (), s32[]{:S(2)}) async-start(), calls=%async_computation.7 | async-start | bytes 8650752 | tf_op jit(solution)/shard_map/all_gather | solution.py:15
  430.5 0.7 copy-start
  431.3 239.9 %all-reduce.6.cloned.1.call-start = ((), (), s32[]{:S(2)}) async-start(), calls=%async_computation.4 | async-start | bytes 262144 | tf_op jit(solution)/shard_map/psum | solution.py:43
  586.0 268.3 %all-gather.17.cloned.1.call-start = ((), (), s32[]{:S(2)}) async-start(), calls=%async_computation.8 | async-start | bytes 8650752 | tf_op jit(solution)/shard_map/all_gather | solution.py:15
  778.6 0.7 copy-start.1
  779.4 239.3 %all-reduce.8.cloned.1.call-start = ((), (), s32[]{:S(2)}) async-start(), calls=%async_computation.5 | async-start | bytes 262144 | tf_op jit(solution)/shard_map/psum | solution.py:43
  1025.3 72.9 %copy-start.3 = (bf16[8192,128]{1,0:T(8,128)(2,1)S(1)}, bf16[8192,128]{1,0:T(8,128)(2,1)}, u32[]{:S(2)}) copy-start(bf16[8192,128]{1,0:T(8,128)(2,1)} %get-tuple-element.548) | copy-start | bytes 6291460
Sparse Core Ops, SparseCore 0:
  8.9 35.8 all-gather.10
  83.4 75.0 all-gather.12
  238.1 84.9 all-reduce.3
  431.4 74.7 all-gather.14
  586.2 84.9 all-reduce.5
  779.5 74.7 all-gather.16
  933.6 84.9 all-reduce.7
